TPU v7x, 32 devices: a whole 2x2x4 slice. The times are simulated.
32 devices in a mesh: row: 4 (over y, x), col: 8 (over z, core).
Axes of the slice: x: 2, y: 2, z: 4, core: 2. Of those that a mesh axis runs over, the one named last changes fastest.
Arguments:
- parent_entries: float32 [16384, 16384], P('row', 'col'), may hold values from -1.5 to 1.5
- children: float32 [6144, 12288], P('row', 'col'), may hold values from -1.5 to 1.5
- shift: float32 [16384], P('row'), may hold values from 24 to 48
- child_map: int32 [2, 96], replicated, may hold values from 0 to 255, as said below
Outputs:
- factored_front: float32 [16384, 16384], P('row', 'col')
Inputs may be any that keep to these rules, and one draw needn't show every extreme that they name: `child_map`: row k sends child k's tiles to distinct parent tiles. For each child and each residue s modulo 4, the entries at positions congruent to s hold at most 8 values of any one residue modulo 4 and at most 8 of any one residue modulo 8, both bounds reached for every s; for each residue v modulo 4, exactly 24 entries of a row are congruent to v.
All inputs are finite; a program needn't handle non-finite values.
Results may differ from a plain program's by a relative error of at most 0.00005.
Values sent between devices are 32-bit elements; how exact they have to be, the bound alone decides.
A program may use at most 448 MiB of HBM per device.

v0:
```python
import jax
import jax.numpy as jnp
from jax import lax
from jax.sharding import PartitionSpec as P

TILE = 64


def from_root(value, axis, source):
    kept = jnp.where(lax.axis_index(axis) == source, value, 0).astype(value.dtype)
    return lax.psum(kept, axis)


def outgoing(block_map, sources, grid_size, own_index, slot_count):
    groups = block_map.shape[0] // sources
    block_table = jnp.take(block_map.reshape(groups, sources), own_index, axis=1)
    target = block_table % grid_size
    ordinal = jnp.arange(groups)
    earlier = (target[:, None] == target[None, :]) & (ordinal[None, :] < ordinal[:, None])
    earlier_count = jnp.sum(earlier.astype(jnp.int32), axis=1)
    picked = (target[None, :, None] == jnp.arange(grid_size)[:, None, None]) & (
        earlier_count[None, :, None] == jnp.arange(slot_count)[None, None, :]
    )
    return jnp.sum(jnp.where(picked, ordinal[None, :, None], 0), axis=1)


def incoming(block_map, sources, grid_size, own_index, slot_count):
    groups = block_map.shape[0] // sources
    block_table = block_map.reshape(groups, sources).T
    to_here = block_table % grid_size == own_index
    counts = to_here.astype(jnp.int32)
    earlier_count = jnp.cumsum(counts, axis=1) - counts
    picked = to_here[:, :, None] & (
        earlier_count[:, :, None] == jnp.arange(slot_count)[None, None, :]
    )
    present = jnp.any(picked, axis=1)
    target = jnp.sum(jnp.where(picked, block_table[:, :, None], 0), axis=1)
    return (present, target)


def compacted(block_map, grid_size, own_index, slot_count, groups):
    present, target = incoming(block_map, grid_size, grid_size, own_index, slot_count)
    flat_present = present.reshape(-1)
    flat_target = target.reshape(-1)
    counts = flat_present.astype(jnp.int32)
    position = jnp.cumsum(counts) - counts
    picked = flat_present[None, :] & (position[None, :] == jnp.arange(groups)[:, None])
    chosen = jnp.sum(jnp.where(picked, jnp.arange(flat_present.shape[0])[None, :], 0), axis=1)
    blocks = jnp.sum(jnp.where(picked, flat_target[None, :], 0), axis=1)
    return (chosen, blocks)


def local(parent_entries, children, shift, child_map):
    rows_here, cols_here = parent_entries.shape
    grid_rows = lax.axis_size("row")
    grid_cols = lax.axis_size("col")
    half_grid = grid_cols // 2
    row_index = lax.axis_index("row")
    col_index = lax.axis_index("col")
    child_now = col_index // half_grid
    half_col = col_index % half_grid
    child_width = children.shape[1]
    groups = children.shape[0] // TILE
    col_groups = child_width // TILE
    slot_count = groups // grid_rows + 2
    own_map = jnp.take(child_map, child_now, axis=0)
    row_blocks = rows_here // TILE
    col_blocks = cols_here // TILE
    col_present = []
    col_targets = []
    for child in range(2):
        present, target = incoming(child_map[child], half_grid, grid_cols, col_index, slot_count)
        col_present.append(present)
        col_targets.append(target)
    col_local = jnp.where(
        jnp.concatenate(col_present, axis=0),
        jnp.concatenate(col_targets, axis=0) // grid_cols,
        col_blocks,
    )
    front_tiles = parent_entries.reshape(row_blocks, TILE, col_blocks, TILE)
    chosen_lists = []
    row_lists = []
    for child in range(2):
        chosen, blocks = compacted(child_map[child], grid_rows, row_index, slot_count, groups)
        chosen_lists.append(chosen)
        row_lists.append(blocks)
    own_chosen = jnp.take(jnp.stack(chosen_lists), child_now, axis=0)
    first_sources = outgoing(own_map, grid_rows, grid_rows, row_index, slot_count)
    child_blocks = children.reshape(groups, TILE, child_width)
    outbound = jnp.take(child_blocks, first_sources.reshape(-1), axis=0).reshape(
        grid_rows, slot_count, TILE, child_width
    )
    arrived = lax.all_to_all(outbound, "row", split_axis=0, concat_axis=0, tiled=True)
    gathered_rows = jnp.take(
        arrived.reshape(grid_rows * slot_count, TILE, child_width), own_chosen, axis=0
    )
    second_sources = outgoing(own_map, half_grid, grid_cols, half_col, slot_count)
    child_tiles = jnp.moveaxis(gathered_rows.reshape(groups, TILE, col_groups, TILE), 2, 0)
    outbound_tiles = jnp.take(child_tiles, second_sources.reshape(-1), axis=0).reshape(
        grid_cols, slot_count, groups, TILE * TILE
    )
    arrived_tiles = lax.all_to_all(outbound_tiles, "col", split_axis=0, concat_axis=0, tiled=True)
    row_local = jnp.repeat(jnp.stack(row_lists), half_grid, axis=0) // grid_rows
    updates = arrived_tiles.reshape(grid_cols, slot_count, groups, TILE, TILE)
    front_tiles = front_tiles.at[row_local[:, None, :], :, col_local[:, :, None], :].add(
        updates, mode="drop"
    )
    row_global = jnp.arange(row_blocks) * grid_rows + row_index
    col_global = jnp.arange(col_blocks) * grid_cols + col_index
    diagonal_tile = row_global[:, None] == col_global[None, :]
    identity = jnp.eye(TILE, dtype=bool)
    shift_tiles = shift.reshape(row_blocks, TILE)
    front_tiles = front_tiles + jnp.where(
        diagonal_tile[:, None, :, None] & identity[None, :, None, :],
        shift_tiles[:, :, None, None],
        0.0,
    )
    parent_front_matrix = front_tiles.reshape(rows_here, cols_here)
    eliminated = TILE * grid_cols
    corner = parent_front_matrix[: 2 * TILE, :TILE].reshape(1, 2 * TILE * TILE)
    corners = lax.all_gather(corner, ("row", "col"), axis=0, tiled=True)
    leading_block = (
        corners.reshape(grid_rows, grid_cols, 2, TILE, TILE)
        .transpose(2, 0, 3, 1, 4)
        .reshape(eliminated, eliminated)
    )
    pivot_block = jnp.linalg.cholesky((leading_block + leading_block.T) * 0.5)
    panel_t = parent_front_matrix[:, :TILE].T
    gathered = lax.all_gather(panel_t, "col", axis=0, tiled=True)
    factor_t = jax.scipy.linalg.solve_triangular(pivot_block, gathered, lower=True)
    own_pivot = jnp.concatenate(
        [
            lax.dynamic_slice_in_dim(pivot_block, row_index * TILE, TILE, 0),
            lax.dynamic_slice_in_dim(pivot_block, (row_index + grid_rows) * TILE, TILE, 0),
        ],
        axis=0,
    )
    factor_t = factor_t.at[:, : 2 * TILE].set(own_pivot.T)
    parity = col_index // grid_rows
    halves = factor_t.reshape(eliminated, row_blocks // 2, 2, TILE)
    picked = lax.dynamic_index_in_dim(halves, parity, axis=2, keepdims=False).reshape(
        eliminated, cols_here
    )
    col_factor = from_root(picked, "row", col_index % grid_rows)
    update = lax.dot_general(
        factor_t,
        col_factor,
        (((0,), (0,)), ((), ())),
        precision=lax.Precision.HIGHEST,
        preferred_element_type=jnp.float32,
    )
    result = parent_front_matrix - update
    panel_out = lax.dynamic_slice_in_dim(factor_t, col_index * TILE, TILE, 0).T
    result = result.at[:, :TILE].set(panel_out)
    result = result.at[: 2 * TILE, TILE:].set(0.0)
    return result


def solution(mesh):
    in_specs = (P("row", "col"), P("row", "col"), P("row"), P())
    out_specs = P("row", "col")
    return jax.shard_map(local, mesh=mesh, in_specs=in_specs, out_specs=out_specs, check_vma=False)
```

profile of v0, /device:TPU:0, one launch (start us, length us, event | category | flops | bytes accessed | tf_op | source)
XLA Modules:
  0.0 1656.2 jit_solution(12107706643401894546)
XLA Ops:
  17.9 11.8 broadcast_select_fusion.1
  39.8 135.1 %all-to-all-done = f32[4,8,64,1536]{3,2,1,0:T(8,128)} async-done(((f32[4,8,64,1536]{3,2,1,0:T(8,128)}), f32[4,8,64,1536]{3,2,1,0:T(8,128)}, u32[]{:S(2)}, u32[]{:S(2)}) %all-to-all-start) | async-done | bytes 12582944 | tf_op jit(solution)/shard_map/all_to_all | solution.py:93
  184.2 14.5 gather.37
  198.7 15.7 fusion
  214.5 29.9 %gather_fusion.2 = f32[64,24,64,64]{3,2,1,0:T(8,128)} fusion(f32[24,24,64,64]{3,2,1,0:T(8,128)} %fusion, s32[1024]{0:T(1024)S(1)} %pad_clamp_fusion), kind=kCustom, calls=%fused_computation.2 | custom fusion | bytes 50331904 | tf_op jit(solution)/shard_map/jit(_take)/gather | solution.py:99
  244.4 40.7 %gather.39 = f32[8,8,24,4096]{3,2,1,0:T(8,128)} reshape(f32[64,24,64,64]{3,2,1,0:T(8,128)} %gather_fusion.2) | data formatting | bytes 50331648 | tf_op jit(solution)/shard_map/jit(_take)/gather | solution.py:99
  285.1 17.8 %broadcast_select_fusion = f32[8,8,24,4096]{3,2,1,0:T(8,128)} fusion(f32[8,8,24,4096]{3,2,1,0:T(8,128)} %gather.39, pred[8,8]{1,0:T(8,128)(4,1)S(1)} %compare_and_fusion), kind=kLoop, calls=%fused_computation.10 | loop fusion | flops 6291456 | bytes 50331712 | tf_op jit(solution)/shard_map/jit(_take)/select_n | solution.py:99
  309.3 11.9 all-gather.6.cloned.1.call-start
  321.2 54.2 %reshape.592 = f32[64,64,32,64]{3,2,1,0:T(8,128)} reshape(f32[4096,2048]{1,0:T(8,128)} %param.12) | data formatting | bytes 67108864 | tf_op jit(solution)/shard_map/reshape | solution.py:80
  376.4 66.1 %copy_add_fusion = f32[64,64,32,64]{3,1,2,0:T(8,128)} fusion(f32[64,64,32,64]{3,2,1,0:T(8,128)} %reshape.592, f32[64,64]{1,0:T(8,128)S(1)} %broadcast_in_dim.220, pred[64,64]{1,0:T(8,128)(4,1)S(1)} %iota_compare_fusion.3, pred[64,32]{1,0:T(8,128)(4,1)S(1)} %broadcast_compare_fusion), kind=kLoop, calls=%fused_computation.6 | loop fusion | flops 25165824 | bytes 67131392 | tf_op jit(solution)/shard_map/add.94
  442.5 410.2 %all-to-all-done.1 = f32[8,8,24,4096]{3,2,1,0:T(8,128)} async-done(((f32[8,8,24,4096]{3,2,1,0:T(8,128)}), f32[8,8,24,4096]{3,2,1,0:T(8,128)}, u32[]{:S(2)}, u32[]{:S(2)}) %all-to-all-start.1) | async-done | bytes 25165856 | tf_op jit(solution)/shard_map/all_to_all | solution.py:102
  852.7 39.6 %reshape.767 = f32[1536,64,64]{2,1,0:T(8,128)} reshape(f32[8,8,24,4096]{3,2,1,0:T(8,128)} %all-to-all-done.1) | data formatting | bytes 50331648 | tf_op jit(solution)/shard_map/reshape | solution.py:104
  892.3 211.9 %scatter_fusion = f32[2048,64,64]{2,1,0:T(8,128)} fusion(f32[2048,64,64]{2,1,0:T(8,128)} %bitcast.1, s32[1536]{0:T(1024)S(1)} %reshape.765, f32[1536,64,64]{2,1,0:T(8,128)} %reshape.767), kind=kCustom, calls=%fused_computation.3 | custom fusion | flops 6291456 | bytes 75503616
  1104.1 56.3 %copy.70 = f32[64,64,32,64]{3,2,1,0:T(8,128)} copy(f32[64,64,32,64]{3,1,2,0:T(8,128)} %bitcast.19) | data formatting | bytes 67108864 | tf_op jit(solution)/shard_map/scatter-add | solution.py:105
  1160.5 56.4 %reshape.601 = f32[4096,2048]{1,0:T(8,128)} reshape(f32[64,64,32,64]{3,2,1,0:T(8,128)} %copy.70) | data formatting | bytes 67108864 | tf_op jit(solution)/shard_map/reshape | solution.py:118
  1222.6 47.6 %all-gather.6.cloned.1.call-done = f32[32,1,8192]{2,1,0:T(1,128)} async-done(((f32[1,1,8192]{2,1,0:T(1,128)}), f32[32,1,8192]{2,1,0:T(1,128)}) %all-gather.6.cloned.1.call-update) | async-done | bytes 1048592 | tf_op jit(solution)/shard_map/all_gather | solution.py:121
  1281.2 11.7 cholesky.104
  1303.5 11.7 cholesky.217
  1325.9 11.7 cholesky.238
  1348.1 11.9 cholesky.255
  1372.8 39.9 %custom-call.34 = f32[4,128,128]{1,2,0:T(8,128)} custom-call(f32[4,128,128]{2,1,0:T(8,128)S(1)} %get-tuple-element.73), custom_call_target="InvertDiagBlocksLowerTriangular" | custom-call | tf_op jit(solution)/shard_map/jit(_solve_triangular)/triangular_solve | solution.py:130
  1460.6 101.6 %all-reduce.3.cloned.1.call-done = f32[512,2048]{0,1:T(8,128)} async-done(((f32[512,2048]{0,1:T(8,128)}), f32[512,2048]{0,1:T(8,128)}) %all-reduce.3.cloned.1.call-update) | async-done | bytes 4194320 | tf_op jit(solution)/shard_map/psum | solution.py:11
  1562.2 61.7 %convolution_subtract_fusion = f32[4096,2048]{1,0:T(8,128)} fusion(f32[4096,2048]{1,0:T(8,128)} %reshape.601, f32[512,4096]{0,1:T(8,128)} %copy-done, f32[512,2048]{0,1:T(8,128)} %all-reduce.3.cloned.1.call-done), kind=kOutput, calls=%fused_computation.9 | convolution fusion | flops 51547996160 | bytes 79691776 | tf_op jit(solution)/shard_map/dot_general | solution.py:145
  1627.3 10.4 scatter.11
  (171 shorter events, 167.0 us)
Async XLA Ops:
  29.8 145.1 %all-to-all-start = ((f32[4,8,64,1536]{3,2,1,0:T(8,128)}), f32[4,8,64,1536]{3,2,1,0:T(8,128)}, u32[]{:S(2)}, u32[]{:S(2)}) async-start(f32[4,8,64,1536]{3,2,1,0:T(8,128)} %broadcast_select_fusion.1), calls=%async_computation | async-start | bytes 25165824 | tf_op jit(solution)/shard_map/all_to_all | solution.py:93
  302.8 549.9 %all-to-all-start.1 = ((f32[8,8,24,4096]{3,2,1,0:T(8,128)}), f32[8,8,24,4096]{3,2,1,0:T(8,128)}, u32[]{:S(2)}, u32[]{:S(2)}) async-start(f32[8,8,24,4096]{3,2,1,0:T(8,128)} %broadcast_select_fusion), calls=%async_computation.1 | async-start | bytes 50331648 | tf_op jit(solution)/shard_map/all_to_all | solution.py:102
  309.3 66.2 %copy-start.4 = (f32[4096]{0:T(1024)S(1)}, f32[4096]{0:T(1024)}, u32[]{:S(2)}) copy-start(f32[4096]{0:T(1024)} %param.14) | copy-start | bytes 49156
  309.3 66.7 %copy-start.6 = (s32[2]{0:T(128)S(1)}, s32[2]{0:T(128)}, u32[]{:S(2)}) copy-start(s32[2]{0:T(128)} %constant.427) | copy-start | bytes 28
  309.3 66.8 %copy-start.5 = (s32[2]{0:T(128)S(1)}, s32[2]{0:T(128)}, u32[]{:S(2)}) copy-start(s32[2]{0:T(128)} %constant.430) | copy-start | bytes 28
  309.3 960.9 %all-gather.6.cloned.1.call-start = ((), (), s32[]{:S(2)}) async-start(), calls=%async_computation.4 | async-start | bytes 1081344 | tf_op jit(solution)/shard_map/all_gather | solution.py:121
  1218.5 194.3 %all-gather.4.cloned.1.call-start = ((), (), s32[]{:S(2)}) async-start(), calls=%async_computation.2 | async-start | bytes 9437184 | tf_op jit(solution)/shard_map/all_gather | solution.py:129
  1221.9 340.3 %all-reduce.3.cloned.1.call-start = ((), (), s32[]{:S(2)}) async-start(), calls=%async_computation.3 | async-start | bytes 8388608 | tf_op jit(solution)/shard_map/psum | solution.py:11
  1440.7 11.2 copy-start.1
  1440.7 11.2 copy-start.2
  1440.7 11.2 copy-start.3
  1452.7 7.2 copy-start.7
  1453.4 3.2 copy-start
Sparse Core Ops, SparseCore 0:
  1218.6 51.5 all-gather.5
  1271.8 81.0 all-gather.3
  1459.4 102.6 all-reduce.2
where the time goes:
time: 1670 us; the launch traced here: 1660 us
  waiting for transfers between devices  695 us (42%)
  other arithmetic  464 us (28%)
  local copies, waits for them, and re-layouts  362 us (22%)
  matrix products  94.6 us (6%)
  starting transfers between devices  24.8 us (1%)
    all_to_all x1, waiting for transfers between devices, local(): lax.all_to_all(outbound_tiles, 'col', split_axis=0, concat_axis=0, tiled=...  410 us
    unnamed x5, other arithmetic  212 us
    all_to_all x1, waiting for transfers between devices, local(): lax.all_to_all(outbound, 'row', split_axis=0, concat_axis=0, tiled=True)  135 us
    psum x1, waiting for transfers between devices, from_root(): return lax.psum(kept, axis)  102 us
    another operation x15, other arithmetic, local(): pivot_block = jnp.linalg.cholesky((leading_block + leading_block.T) * 0.5)  79.2 us
    another operation x10, other arithmetic  74.7 us
    gather x2, local copies, waits for them, and re-layouts, local(): jnp.take(child_tiles, second_sources.reshape(-1), axis=0)  70.6 us
    dot_general x1, matrix products, local(): lax.dot_general(factor_t, col_factor, (((0,), (0,)), ((), ())), precision...  61.7 us
  transfers between devices with their start and end apart: 5, of which 4 were waited for; matrix products, arithmetic and copies ran while one was open for 16% of the time, Pallas kernels for 0%

commit v1 on v0

v1 whole, which is shorter than its diff:
```python
import jax
import jax.numpy as jnp
from jax import lax
from jax.experimental import pallas as pl
from jax.experimental.pallas import tpu as pltpu
from jax.sharding import PartitionSpec as P

TILE = 64


def from_root(value, axis, source):
    kept = jnp.where(lax.axis_index(axis) == source, value, 0).astype(value.dtype)
    return lax.psum(kept, axis)


def outgoing(block_map, sources, grid_size, own_index, slot_count):
    groups = block_map.shape[0] // sources
    block_table = jnp.take(block_map.reshape(groups, sources), own_index, axis=1)
    target = block_table % grid_size
    ordinal = jnp.arange(groups)
    earlier = (target[:, None] == target[None, :]) & (ordinal[None, :] < ordinal[:, None])
    earlier_count = jnp.sum(earlier.astype(jnp.int32), axis=1)
    picked = (target[None, :, None] == jnp.arange(grid_size)[:, None, None]) & (
        earlier_count[None, :, None] == jnp.arange(slot_count)[None, None, :]
    )
    return jnp.sum(jnp.where(picked, ordinal[None, :, None], 0), axis=1)


def incoming(block_map, sources, grid_size, own_index, slot_count):
    groups = block_map.shape[0] // sources
    block_table = block_map.reshape(groups, sources).T
    to_here = block_table % grid_size == own_index
    counts = to_here.astype(jnp.int32)
    earlier_count = jnp.cumsum(counts, axis=1) - counts
    picked = to_here[:, :, None] & (
        earlier_count[:, :, None] == jnp.arange(slot_count)[None, None, :]
    )
    present = jnp.any(picked, axis=1)
    target = jnp.sum(jnp.where(picked, block_table[:, :, None], 0), axis=1)
    return (present, target)


def compacted(block_map, grid_size, own_index, slot_count, groups):
    present, target = incoming(block_map, grid_size, grid_size, own_index, slot_count)
    flat_present = present.reshape(-1)
    flat_target = target.reshape(-1)
    counts = flat_present.astype(jnp.int32)
    position = jnp.cumsum(counts) - counts
    picked = flat_present[None, :] & (position[None, :] == jnp.arange(groups)[:, None])
    chosen = jnp.sum(jnp.where(picked, jnp.arange(flat_present.shape[0])[None, :], 0), axis=1)
    blocks = jnp.sum(jnp.where(picked, flat_target[None, :], 0), axis=1)
    return (chosen, blocks)


CHUNKS = 4


def lane_half(value, column, half):
    return jnp.where(column % 2 == half, value, pltpu.roll(value, TILE, 1))


def lane_pair(column):
    return pl.ds(pl.multiple_of((column // 2) * (2 * TILE), 2 * TILE), 2 * TILE)


def shuffle_columns(source, row_table, major_table, column_table, dests):
    majors, _, _, width = source.shape
    rows = row_table.shape[0]
    count = column_table.shape[0]
    per_dest = count // dests

    def body(row_ref, major_ref, column_ref, in_ref, out_ref):
        low = lax.broadcasted_iota(jnp.int32, (TILE, 2 * TILE), 1) < TILE
        for first in range(0, count, 2):
            halves = []
            for half in range(2):
                column = column_ref[first + half]
                value = in_ref[major_ref[first + half], 0, :, lane_pair(column)]
                halves.append(lane_half(value, column, half))
            place = first % per_dest
            out_ref[first // per_dest, 0, :, place * TILE : (place + 2) * TILE] = jnp.where(
                low, halves[0], halves[1]
            )

    return pl.pallas_call(
        body,
        out_shape=jax.ShapeDtypeStruct((dests, rows, TILE, per_dest * TILE), jnp.float32),
        grid_spec=pltpu.PrefetchScalarGridSpec(
            num_scalar_prefetch=3,
            grid=(rows,),
            in_specs=[
                pl.BlockSpec((majors, 1, TILE, width), lambda j, row, major, column: (0, row[j], 0, 0))
            ],
            out_specs=pl.BlockSpec(
                (dests, 1, TILE, per_dest * TILE), lambda j, row, major, column: (0, j, 0, 0)
            ),
        ),
        cost_estimate=pl.CostEstimate(
            flops=0, transcendentals=0, bytes_accessed=8 * rows * TILE * count * TILE
        ),
    )(row_table, major_table, column_table, source)


def extend_add(front, update, row_table, column_table):
    rows, _, width = update.shape
    cols_here = front.shape[1]

    def body(row_ref, column_ref, front_ref, update_ref, out_ref):
        out_ref[...] = front_ref[...]

        @pl.when(row_ref[pl.program_id(0)] >= 2)
        def _():
            upper = lax.broadcasted_iota(jnp.int32, (TILE, 2 * TILE), 1) // TILE
            for q in range(width // TILE):
                column = column_ref[q]

                @pl.when(column >= 1)
                def _():
                    first = (q // 2) * 2 * TILE
                    value = lane_half(update_ref[0, :, first : first + 2 * TILE], column, q % 2)
                    out_ref[:, lane_pair(column)] += jnp.where(upper == column % 2, value, 0.0)

    return pl.pallas_call(
        body,
        out_shape=jax.ShapeDtypeStruct(front.shape, jnp.float32),
        grid_spec=pltpu.PrefetchScalarGridSpec(
            num_scalar_prefetch=2,
            grid=(rows,),
            in_specs=[
                pl.BlockSpec((TILE, cols_here), lambda j, row, column: (row[j], 0)),
                pl.BlockSpec((1, TILE, width), lambda j, row, column: (j, 0, 0)),
            ],
            out_specs=pl.BlockSpec((TILE, cols_here), lambda j, row, column: (row[j], 0)),
        ),
        input_output_aliases={2: 0},
        cost_estimate=pl.CostEstimate(
            flops=rows * TILE * width,
            transcendentals=0,
            bytes_accessed=4 * rows * TILE * (2 * cols_here + width),
        ),
    )(row_table, column_table, front, update)


def local(parent_entries, children, shift, child_map):
    rows_here, cols_here = parent_entries.shape
    grid_rows = lax.axis_size("row")
    grid_cols = lax.axis_size("col")
    half_grid = grid_cols // 2
    row_index = lax.axis_index("row")
    col_index = lax.axis_index("col")
    child_now = col_index // half_grid
    half_col = col_index % half_grid
    child_width = children.shape[1]
    groups = children.shape[0] // TILE
    slot_count = groups // grid_rows + 2
    col_slots = slot_count + slot_count % 2
    row_blocks = rows_here // TILE
    own_map = jnp.take(child_map, child_now, axis=0)

    chosen_lists, row_lists, col_chosen, col_lists = [], [], [], []
    for child in range(2):
        chosen, blocks = compacted(child_map[child], grid_rows, row_index, slot_count, groups)
        chosen_lists.append(chosen)
        row_lists.append(blocks // grid_rows)
        chosen, blocks = compacted(child_map[child], half_grid, half_col, col_slots, groups)
        col_chosen.append(chosen)
        col_lists.append(jnp.where(blocks % grid_cols == col_index, blocks // grid_cols, -1))
    row_lists = jnp.stack(row_lists)
    col_lists = jnp.stack(col_lists)
    own_chosen = jnp.take(jnp.stack(chosen_lists), child_now, axis=0)
    own_col_chosen = jnp.take(jnp.stack(col_chosen), child_now, axis=0)

    first_sources = outgoing(own_map, grid_rows, grid_rows, row_index, slot_count)
    child_blocks = children.reshape(groups, TILE, child_width)
    outbound = jnp.take(child_blocks, first_sources.reshape(-1), axis=0, mode="clip").reshape(
        grid_rows, slot_count, TILE, child_width
    )
    arrived = lax.all_to_all(outbound, "row", split_axis=0, concat_axis=0, tiled=True)
    arrived = arrived.reshape(1, grid_rows * slot_count, TILE, child_width)

    owned = jnp.take(own_map.reshape(groups, half_grid), half_col, axis=1)
    leads = owned[:, None] == jnp.arange(grid_cols)[None, :]
    lead_source = jnp.sum(jnp.where(leads, jnp.arange(groups)[:, None], 0), axis=0)
    lead_strips = shuffle_columns(arrived, own_chosen, jnp.zeros_like(lead_source), lead_source, 1)
    lead_strips = lead_strips.reshape(groups * TILE, grid_cols * TILE).T.reshape(
        grid_cols, TILE, groups * TILE
    )
    lead_strips = jnp.where(jnp.any(leads, axis=0)[:, None, None], lead_strips, 0.0)
    lead_arrived = lax.all_to_all(lead_strips, "col", split_axis=0, concat_axis=0, tiled=True)

    second_sources = outgoing(own_map, half_grid, half_grid, half_col, col_slots).reshape(-1)
    halves = [list(range(half_grid)), list(range(half_grid, grid_cols))]
    swap = [(c, (c + half_grid) % grid_cols) for c in range(grid_cols)]
    step = groups // CHUNKS
    sends = []
    for chunk in range(CHUNKS):
        part = shuffle_columns(
            arrived,
            own_chosen[chunk * step : (chunk + 1) * step],
            jnp.zeros_like(second_sources),
            second_sources,
            half_grid,
        )
        sends.append(part)
    held = lax.optimization_barrier((lead_arrived, *sends))
    lead_arrived, sends = held[0], held[1:]
    own_parts = []
    for part in sends:
        got = lax.all_to_all(
            part, "col", split_axis=0, concat_axis=0, tiled=True, axis_index_groups=halves
        )
        own = shuffle_columns(
            got, jnp.arange(step), own_col_chosen // col_slots, own_col_chosen % col_slots, 1
        )[0]
        own_parts.append(own)

    lead_arrived = jnp.sum(lead_arrived.reshape(2, half_grid, TILE, groups * TILE), axis=1)
    row_ids = (
        (jnp.arange(row_blocks) * grid_rows + row_index)[:, None] * TILE + jnp.arange(TILE)
    ).reshape(rows_here)
    col_ids = (
        (jnp.arange(cols_here // TILE) * grid_cols + col_index)[:, None] * TILE + jnp.arange(TILE)
    ).reshape(cols_here)
    panel = parent_entries[:, :TILE] + jnp.where(
        row_ids[:, None] == col_ids[None, :TILE], shift[:, None], 0.0
    )
    panel = panel.reshape(row_blocks, TILE, TILE)
    for child in range(2):
        hits = jnp.arange(row_blocks)[:, None] == row_lists[child][None, :]
        source = jnp.sum(jnp.where(hits, jnp.arange(groups)[None, :], 0), axis=1)
        strip = lead_arrived[child].T.reshape(groups, TILE, TILE)
        strip = jnp.take(strip, source, axis=0, mode="clip")
        panel = panel + jnp.where(jnp.any(hits, axis=1)[:, None, None], strip, 0.0)
    panel = panel.reshape(rows_here, TILE)

    eliminated = TILE * grid_cols
    corner = panel[: 2 * TILE].reshape(1, 2 * TILE * TILE)
    corners = lax.all_gather(corner, ("row", "col"), axis=0, tiled=True)
    leading_block = (
        corners.reshape(grid_rows, grid_cols, 2, TILE, TILE)
        .transpose(2, 0, 3, 1, 4)
        .reshape(eliminated, eliminated)
    )
    gathered = lax.all_gather(panel.T, "col", axis=0, tiled=True)
    parity = col_index // grid_rows
    halves_t = gathered.reshape(eliminated, row_blocks // 2, 2, TILE)
    picked = lax.dynamic_index_in_dim(halves_t, parity, axis=2, keepdims=False).reshape(
        eliminated, cols_here
    )
    picked = from_root(picked, "row", col_index % grid_rows)
    half = CHUNKS // 2
    held = lax.optimization_barrier((leading_block, *own_parts[:half]))
    leading_block, own_parts[:half] = held[0], held[1:]
    pivot_block = jnp.linalg.cholesky((leading_block + leading_block.T) * 0.5)
    other_parts = [lax.ppermute(own, "col", swap) for own in own_parts[:half]]
    held = lax.optimization_barrier((pivot_block, other_parts[0], *own_parts[half:]))
    pivot_block, other_parts[0], own_parts[half:] = held[0], held[1], held[2:]
    other_parts += [lax.ppermute(own, "col", swap) for own in own_parts[half:]]
    solved = jax.scipy.linalg.solve_triangular(
        pivot_block, jnp.concatenate([gathered, picked], axis=1), lower=True
    )
    held = lax.optimization_barrier((solved, *other_parts[1:-1]))
    solved, other_parts[1:-1] = held[0], held[1:]
    factor_t, col_factor = solved[:, :rows_here], solved[:, rows_here:]
    own_pivot = jnp.concatenate(
        [
            lax.dynamic_slice_in_dim(pivot_block, row_index * TILE, TILE, 0),
            lax.dynamic_slice_in_dim(pivot_block, (row_index + grid_rows) * TILE, TILE, 0),
        ],
        axis=0,
    )
    factor_t = factor_t.at[:, : 2 * TILE].set(own_pivot.T)
    update = lax.dot_general(
        factor_t,
        col_factor,
        (((0,), (0,)), ((), ())),
        precision=lax.Precision.HIGH,
        preferred_element_type=jnp.float32,
    )
    result = parent_entries - update
    result = result + jnp.where(row_ids[:, None] == col_ids[None, :], shift[:, None], 0.0)
    panel_out = lax.dynamic_slice_in_dim(factor_t, col_index * TILE, TILE, 0).T
    result = jnp.where((jnp.arange(rows_here) < 2 * TILE)[:, None], 0.0, result)
    result = result.at[:, :TILE].set(panel_out)

    own_rows = jnp.take(row_lists, child_now, axis=0)
    other_rows = jnp.take(row_lists, 1 - child_now, axis=0)
    own_cols = jnp.take(col_lists, child_now, axis=0)
    other_cols = jnp.take(col_lists, 1 - child_now, axis=0)
    for parts, rows, cols in ((own_parts, own_rows, own_cols), (other_parts, other_rows, other_cols)):
        for chunk, part in enumerate(parts):
            result = extend_add(result, part, rows[chunk * step : (chunk + 1) * step], cols)
    return result


def solution(mesh):
    in_specs = (P("row", "col"), P("row", "col"), P("row"), P())
    out_specs = P("row", "col")
    return jax.shard_map(local, mesh=mesh, in_specs=in_specs, out_specs=out_specs, check_vma=False)
```

time: 1670 us -> 1060 us (0.63)
  other arithmetic: 464 us -> 163 us
  waiting for transfers between devices: 695 us -> 402 us
  local copies, waits for them, and re-layouts: 362 us -> 114 us
  Pallas kernels: 0 us -> 155 us
  blocking collectives: 0 us -> 80.4 us
    all_to_all x1 -> x4, waiting for transfers between devices: 410 us -> 122 us  [the longest x3 85.8 us: local(): lax.all_to_all(part, 'col', split_axis=0, concat_axis=0, tiled=True, axis...]
    unnamed x5 -> x1, other arithmetic: 212 us -> 0.01 us
    pallas_call x0 -> x17, Pallas kernels: none -> 155 us  [the longest x8 85.7 us: extend_add(): pl.pallas_call(body, out_shape=jax.ShapeDtypeStruct(front.shape, jnp.floa...]
    reshape x5 -> x2, local copies, waits for them, and re-layouts: 150 us -> 3.05 us  [the longest x1 2.37 us: local(): lead_strips.reshape(groups * TILE, grid_cols * TILE)]
    ppermute x0 -> x4, waiting for transfers between devices: none -> 144 us  [the longest x2 85.3 us: local(): other_parts += [lax.ppermute(own, 'col', swap) for own in own_parts[half:]]]
    psum x1, waiting for transfers between devices: 102 us -> 0.01 us  [from_root(): return lax.psum(kept, axis)]
    gather x5, local copies, waits for them, and re-layouts: 104 us -> 17.4 us  [the longest x1 9.82 us: local(): jnp.take(child_blocks, first_sources.reshape(-1), axis=0, mode='clip')]
    all_to_all x0 -> x1, blocking collectives: none -> 80.4 us  [local(): lax.all_to_all(part, 'col', split_axis=0, concat_axis=0, tiled=True, axis...]
  transfers between devices with their start and end apart: 5 -> 12, of which waited for: 4 -> 6; matrix products, arithmetic and copies ran while one was open for 16% -> 32% of each run, Pallas kernels for 0% -> 12%
where the time goes in v1:
time: 1060 us; the launch traced here: 1050 us
  waiting for transfers between devices  402 us (38%)
  other arithmetic  163 us (15%)
  Pallas kernels  155 us (15%)
  local copies, waits for them, and re-layouts  114 us (11%)
  matrix products  85 us (8%)
  blocking collectives  80.4 us (8%)
  starting transfers between devices  29.9 us (3%)
  between operations  16.8 us (2%)
    all_to_all x1, waiting for transfers between devices, local(): lax.all_to_all(outbound, 'row', split_axis=0, concat_axis=0, tiled=True)  136 us
    another operation x15, other arithmetic, local(): pivot_block = jnp.linalg.cholesky((leading_block + leading_block.T) * 0.5)  87 us
    all_to_all x3, waiting for transfers between devices, local(): lax.all_to_all(part, 'col', split_axis=0, concat_axis=0, tiled=True, axis...  85.8 us
    pallas_call x8, Pallas kernels, extend_add(): pl.pallas_call(body, out_shape=jax.ShapeDtypeStruct(front.shape, jnp.floa...  85.7 us
    ppermute x2, waiting for transfers between devices, local(): other_parts += [lax.ppermute(own, 'col', swap) for own in own_parts[half:]]  85.3 us
    all_to_all x1, blocking collectives, local(): lax.all_to_all(part, 'col', split_axis=0, concat_axis=0, tiled=True, axis...  80.4 us
    pallas_call x9, Pallas kernels, shuffle_columns(): pl.pallas_call(body, out_shape=jax.ShapeDtypeStruct((dests, rows, TILE, p...  68.8 us
    ppermute x2, waiting for transfers between devices, local(): other_parts = [lax.ppermute(own, 'col', swap) for own in own_parts[:half]]  58.5 us
  transfers between devices with their start and end apart: 12, of which 6 were waited for; matrix products, arithmetic and copies ran while one was open for 32% of the time, Pallas kernels for 12%

profile of v1, /device:TPU:0, one launch (start us, length us, event | category | flops | bytes accessed | tf_op | source)
XLA Modules:
  0.0 1045.2 jit_solution(14268113478748891668)
XLA Ops:
  28.8 135.8 %all-to-all-done = f32[4,8,64,1536]{3,2,1,0:T(8,128)} async-done(((f32[4,8,64,1536]{3,2,1,0:T(8,128)}), f32[4,8,64,1536]{3,2,1,0:T(8,128)}, u32[]{:S(2)}, u32[]{:S(2)}) %all-to-all-start) | async-done | bytes 12582944 | tf_op jit(solution)/shard_map/all_to_all | solution.py:178
  165.2 16.6 %shard_map.46 = f32[1,24,64,512]{3,2,1,0:T(8,128)} custom-call(s32[24]{0:T(128)} %fusion.62.row_ref, s32[8]{0:T(128)} %broadcast_15_major_ref.2.major_ref, s32[8]{0:T(128)} %select_reduce_fusion.22.column_ref, f32[1,32,64,1536]{3,2,1,0:T(8,128)} %bitcast.17.in_ref), custom_call_target="tpu_custom_call" | custom-call | bytes 6291456 | tf_op jit(solution)/shard_map/pallas_call | solution.py:85
  227.1 35.7 %all-to-all-done.1 = f32[8,64,1536]{2,1,0:T(8,128)S(1)} async-done(((f32[8,64,1536]{2,1,0:T(8,128)}), f32[8,64,1536]{2,1,0:T(8,128)S(1)}, u32[]{:S(2)}, u32[]{:S(2)}) %all-to-all-start.1) | async-done | bytes 3145760 | tf_op jit(solution)/shard_map/all_to_all | solution.py:189
  284.4 28.9 %all-to-all-done.2.in_ref = f32[4,6,64,512]{3,2,1,0:T(8,128)S(1)} async-done(((f32[4,6,64,512]{3,2,1,0:T(8,128)}), f32[4,6,64,512]{3,2,1,0:T(8,128)S(1)}, u32[]{:S(2)}, u32[]{:S(2)}) %all-to-all-start.2) | async-done | bytes 3145760 | tf_op jit(solution)/shard_map/all_to_all | solution.py:209
  313.2 80.4 %all_to_all.30.in_ref = f32[4,6,64,512]{3,2,1,0:T(8,128)} all-to-all(f32[4,6,64,512]{3,2,1,0:T(8,128)} %shard_map.48), channel_id=1, replica_groups={{0,1,2,3},{4,5,6,7},{8,9,10,11},{12,13,14,15},{16,17,18,19},{20,21,22,2..., dimensions={0} | all-to-all | bytes 6291456 | tf_op jit(solution)/shard_map/all_to_all | solution.py:209
  402.4 56.9 %all-to-all-done.4.in_ref = f32[4,6,64,512]{3,2,1,0:T(8,128)S(1)} async-done(((f32[4,6,64,512]{3,2,1,0:T(8,128)}), f32[4,6,64,512]{3,2,1,0:T(8,128)S(1)}, u32[]{:S(2)}, u32[]{:S(2)}) %all-to-all-start.4) | async-done | bytes 3145760 | tf_op jit(solution)/shard_map/all_to_all | solution.py:209
  496.5 11.7 %cholesky.104 = f32[128,128]{1,0:T(8,128)S(1)} custom-call(f32[128,128]{1,0:T(8,128)S(1)} %cholesky.266), custom_call_target="Cholesky" | custom-call | tf_op jit(solution)/shard_map/jit(cholesky)/cholesky | solution.py:254
  521.9 11.7 %cholesky.217 = f32[128,128]{1,0:T(8,128)S(1)} custom-call(f32[128,128]{1,0:T(8,128)S(1)} %cholesky.270), custom_call_target="Cholesky" | custom-call | tf_op jit(solution)/shard_map/jit(cholesky)/cholesky | solution.py:254
  566.8 13.2 %cholesky.238 = f32[128,128]{1,0:T(8,128)} custom-call(f32[128,128]{1,0:T(8,128)} %cholesky.275), custom_call_target="Cholesky" | custom-call | tf_op jit(solution)/shard_map/jit(cholesky)/cholesky | solution.py:254
  582.0 11.3 %custom-call.33 = f32[1,128,128]{1,2,0:T(8,128)} custom-call(f32[1,128,128]{2,1,0:T(8,128)} %get-tuple-element.148), custom_call_target="InvertDiagBlocksLowerTriangular" | custom-call | tf_op jit(solution)/shard_map/jit(cholesky)/cholesky | solution.py:254
  595.5 11.7 %cholesky.255 = f32[128,128]{1,0:T(8,128)S(1)} custom-call(f32[128,128]{1,0:T(8,128)S(1)} %convolution_subtract_fusion.4), custom_call_target="Cholesky" | custom-call | tf_op jit(solution)/shard_map/jit(cholesky)/cholesky | solution.py:254
  631.4 58.5 %collective-permute-done.update_ref = f32[6,64,1536]{2,1,0:T(8,128)} collective-permute-done((f32[6,64,1536]{2,1,0:T(8,128)S(1)}, f32[6,64,1536]{2,1,0:T(8,128)}, u32[]{:S(2)}, u32[]{:S(2)}) %collective-permute-start) | collective-permute-done | bytes 2359328 | tf_op jit(solution)/shard_map/ppermute | solution.py:255
  700.2 41.1 %custom-call.34 = f32[4,128,128]{1,2,0:T(8,128)} custom-call(f32[4,128,128]{2,1,0:T(8,128)} %get-tuple-element.92), custom_call_target="InvertDiagBlocksLowerTriangular" | custom-call | tf_op jit(solution)/shard_map/jit(_solve_triangular)/triangular_solve | solution.py:259
  809.6 85.3 %collective-permute-done.2.update_ref = f32[6,64,1536]{2,1,0:T(8,128)} collective-permute-done((f32[6,64,1536]{2,1,0:T(8,128)}, f32[6,64,1536]{2,1,0:T(8,128)}, u32[]{:S(2)}, u32[]{:S(2)}) %collective-permute-start.2) | collective-permute-done | bytes 2359328 | tf_op jit(solution)/shard_map/ppermute | solution.py:258
  900.5 38.1 %add_select_fusion = f32[4096,2048]{1,0:T(8,128)} fusion(f32[4096,2048]{1,0:T(8,128)} %param.12, f32[4096]{0:T(1024)S(1)} %copy-done.16, s32[2048]{0:T(1024)S(1)} %copy-done.17, s32[4096]{0:T(1024)S(1)} %add.259, pred[4096]{0:T(1024)(128)(4,1)S(1)} %copy-done.18, f32[512,4096]{0,1:T(8,128)} %fusion.20, f32[512,6144]{0,1:T(8,128)} %copy-done.1), kind=kOutput, calls=%fused_computation.5 | convolution fusion | flops 25811746816 | bytes 79736832 | tf_op jit(solution)/shard_map/dot_general | solution.py:273
  942.1 10.4 scatter.9.front_ref
  952.5 10.5 %shard_map.55.front_ref = f32[4096,2048]{1,0:T(8,128)} custom-call(s32[6]{0:T(128)} %get-tuple-element.167.row_ref, s32[24]{0:T(128)} %get-tuple-element.159.column_ref, f32[4096,2048]{1,0:T(8,128)} %scatter.9.front_ref, f32[6,64,1536]{2,1,0:T(8,128)} %bitcast.175), custom_call_target="tpu_custom_call", output_to_operand_aliasing={{}: (2, {})} | custom-call | flops 589824 | bytes 8650752 | tf_op jit(solution)/shard_map/pallas_call | solution.py:123
  963.0 10.5 %shard_map.56.front_ref = f32[4096,2048]{1,0:T(8,128)} custom-call(s32[6]{0:T(128)} %get-tuple-element.168.row_ref, s32[24]{0:T(128)} %get-tuple-element.159.column_ref, f32[4096,2048]{1,0:T(8,128)} %shard_map.55.front_ref, f32[6,64,1536]{2,1,0:T(8,128)} %bitcast.178), custom_call_target="tpu_custom_call", output_to_operand_aliasing={{}: (2, {})} | custom-call | flops 589824 | bytes 8650752 | tf_op jit(solution)/shard_map/pallas_call | solution.py:123
  973.5 10.5 %shard_map.57.front_ref = f32[4096,2048]{1,0:T(8,128)} custom-call(s32[6]{0:T(128)} %get-tuple-element.169.row_ref, s32[24]{0:T(128)} %get-tuple-element.159.column_ref, f32[4096,2048]{1,0:T(8,128)} %shard_map.56.front_ref, f32[6,64,1536]{2,1,0:T(8,128)} %bitcast.182), custom_call_target="tpu_custom_call", output_to_operand_aliasing={{}: (2, {})} | custom-call | flops 589824 | bytes 8650752 | tf_op jit(solution)/shard_map/pallas_call | solution.py:123
  984.0 10.5 %shard_map.58.front_ref = f32[4096,2048]{1,0:T(8,128)} custom-call(s32[6]{0:T(128)} %get-tuple-element.170.row_ref, s32[24]{0:T(128)} %get-tuple-element.159.column_ref, f32[4096,2048]{1,0:T(8,128)} %shard_map.57.front_ref, f32[6,64,1536]{2,1,0:T(8,128)} %bitcast.180), custom_call_target="tpu_custom_call", output_to_operand_aliasing={{}: (2, {})} | custom-call | flops 589824 | bytes 8650752 | tf_op jit(solution)/shard_map/pallas_call | solution.py:123
  994.5 10.9 %shard_map.59.front_ref = f32[4096,2048]{1,0:T(8,128)} custom-call(s32[6]{0:T(128)} %get-tuple-element.171.row_ref, s32[24]{0:T(128)} %get-tuple-element.160.column_ref, f32[4096,2048]{1,0:T(8,128)} %shard_map.58.front_ref, f32[6,64,1536]{2,1,0:T(8,128)} %collective-permute-done.update_ref), custom_call_target="tpu_custom_call", output_to_operand_aliasing={{}: (2, {})} | custom-call | flops 589824 | bytes 8650752 | tf_op jit(solution)/shard_map/pallas_call | solution.py:123
  1005.4 10.9 %shard_map.60.front_ref = f32[4096,2048]{1,0:T(8,128)} custom-call(s32[6]{0:T(128)} %get-tuple-element.172.row_ref, s32[24]{0:T(128)} %get-tuple-element.160.column_ref, f32[4096,2048]{1,0:T(8,128)} %shard_map.59.front_ref, f32[6,64,1536]{2,1,0:T(8,128)} %collective-permute-done.1.update_ref), custom_call_target="tpu_custom_call", output_to_operand_aliasing={{}: (2, {})} | custom-call | flops 589824 | bytes 8650752 | tf_op jit(solution)/shard_map/pallas_call | solution.py:123
  1016.3 11.0 %shard_map.61.front_ref = f32[4096,2048]{1,0:T(8,128)} custom-call(s32[6]{0:T(128)} %get-tuple-element.173.row_ref, s32[24]{0:T(128)} %get-tuple-element.160.column_ref, f32[4096,2048]{1,0:T(8,128)} %shard_map.60.front_ref, f32[6,64,1536]{2,1,0:T(8,128)} %collective-permute-done.2.update_ref), custom_call_target="tpu_custom_call", output_to_operand_aliasing={{}: (2, {})} | custom-call | flops 589824 | bytes 8650752 | tf_op jit(solution)/shard_map/pallas_call | solution.py:123
  1027.3 10.9 %shard_map.62 = f32[4096,2048]{1,0:T(8,128)} custom-call(s32[6]{0:T(128)} %get-tuple-element.174.row_ref, s32[24]{0:T(128)} %get-tuple-element.160.column_ref, f32[4096,2048]{1,0:T(8,128)} %shard_map.61.front_ref, f32[6,64,1536]{2,1,0:T(8,128)} %collective-permute-done.3.update_ref), custom_call_target="tpu_custom_call", output_to_operand_aliasing={{}: (2, {})} | custom-call | flops 589824 | bytes 8650752 | tf_op jit(solution)/shard_map/pallas_call | solution.py:123
  (263 shorter events, 305.3 us)
Async XLA Ops:
  19.5 145.1 %all-to-all-start = ((f32[4,8,64,1536]{3,2,1,0:T(8,128)}), f32[4,8,64,1536]{3,2,1,0:T(8,128)}, u32[]{:S(2)}, u32[]{:S(2)}) async-start(f32[4,8,64,1536]{3,2,1,0:T(8,128)} %bitcast.167), calls=%async_computation | async-start | bytes 25165824 | tf_op jit(solution)/shard_map/all_to_all | solution.py:178
  186.3 76.6 %all-to-all-start.1 = ((f32[8,64,1536]{2,1,0:T(8,128)}), f32[8,64,1536]{2,1,0:T(8,128)S(1)}, u32[]{:S(2)}, u32[]{:S(2)}) async-start(f32[8,64,1536]{2,1,0:T(8,128)} %broadcast_select_fusion), calls=%async_computation.1 | async-start | bytes 6291456 | tf_op jit(solution)/shard_map/all_to_all | solution.py:189
  193.1 6.5 copy-start.14
  271.3 41.9 %all-to-all-start.2 = ((f32[4,6,64,512]{3,2,1,0:T(8,128)}), f32[4,6,64,512]{3,2,1,0:T(8,128)S(1)}, u32[]{:S(2)}, u32[]{:S(2)}) async-start(f32[4,6,64,512]{3,2,1,0:T(8,128)} %shard_map.47), calls=%async_computation.2 | async-start | bytes 6291456 | tf_op jit(solution)/shard_map/all_to_all | solution.py:209
  275.1 193.4 %all-gather.6.cloned.1.call-start = ((), (), s32[]{:S(2)}) async-start(), calls=%async_computation.8 | async-start | bytes 1081344 | tf_op jit(solution)/shard_map/all_gather | solution.py:238
  283.6 261.9 %all-gather.4.cloned.1.call-start = ((), (), s32[]{:S(2)}) async-start(), calls=%async_computation.6 | async-start | bytes 9437184 | tf_op jit(solution)/shard_map/all_gather | solution.py:244
  313.2 80.4 %copy-start.6 = (f32[4,6,64,512]{3,2,1,0:T(8,128)}, f32[4,6,64,512]{3,2,1,0:T(8,128)S(1)}, u32[]{:S(2)}) copy-start(f32[4,6,64,512]{3,2,1,0:T(8,128)S(1)} %all-to-all-done.2.in_ref) | copy-start | bytes 9437188
  393.7 65.7 %all-to-all-start.4 = ((f32[4,6,64,512]{3,2,1,0:T(8,128)}), f32[4,6,64,512]{3,2,1,0:T(8,128)S(1)}, u32[]{:S(2)}, u32[]{:S(2)}) async-start(f32[4,6,64,512]{3,2,1,0:T(8,128)} %shard_map.49), calls=%async_computation.4 | async-start | bytes 6291456 | tf_op jit(solution)/shard_map/all_to_all | solution.py:209
  461.1 163.1 %all-to-all-start.5 = ((f32[4,6,64,512]{3,2,1,0:T(8,128)}), f32[4,6,64,512]{3,2,1,0:T(8,128)}, u32[]{:S(2)}, u32[]{:S(2)}) async-start(f32[4,6,64,512]{3,2,1,0:T(8,128)} %shard_map.50), calls=%async_computation.5 | async-start | bytes 6291456 | tf_op jit(solution)/shard_map/all_to_all | solution.py:209
  465.7 287.2 %all-reduce.3.cloned.1.call-start = ((), (), s32[]{:S(2)}) async-start(), calls=%async_computation.7 | async-start | bytes 8388608 | tf_op jit(solution)/shard_map/psum | solution.py:13
  493.9 39.7 %copy-start.7 = (f32[1,6,64,1536]{3,2,1,0:T(8,128)S(1)}, f32[1,6,64,1536]{3,2,1,0:T(8,128)}, u32[]{:S(2)}) copy-start(f32[1,6,64,1536]{3,2,1,0:T(8,128)} %shard_map.51) | copy-start | bytes 7077892
  533.6 156.2 %collective-permute-start = (f32[6,64,1536]{2,1,0:T(8,128)S(1)}, f32[6,64,1536]{2,1,0:T(8,128)}, u32[]{:S(2)}, u32[]{:S(2)}) collective-permute-start(f32[6,64,1536]{2,1,0:T(8,128)S(1)} %bitcast.176), channel_id=1, source_target_pairs={{0,4},{1,5},{2,6},{3,7},{4,0},{5,1},{6,2},{7,3},{8,12},{9,13},{10,... | collective-permute-start | bytes 7077896 | tf_op jit(solution)/shard_map/ppermute | solution.py:255
  607.2 202.4 %collective-permute-start.1 = (f32[6,64,1536]{2,1,0:T(8,128)}, f32[6,64,1536]{2,1,0:T(8,128)}, u32[]{:S(2)}, u32[]{:S(2)}) collective-permute-start(f32[6,64,1536]{2,1,0:T(8,128)} %bitcast.177), channel_id=1, source_target_pairs={{0,4},{1,5},{2,6},{3,7},{4,0},{5,1},{6,2},{7,3},{8,12},{9,13},{10,... | collective-permute-start | bytes 7077896 | tf_op jit(solution)/shard_map/ppermute | solution.py:255
  631.2 58.8 %copy-start.19 = (s32[4]{0:T(128)S(1)}, s32[4]{0:T(128)}, u32[]{:S(2)}) copy-start(s32[4]{0:T(128)} %iota_multiply_fusion) | copy-start | bytes 52
  631.4 58.5 %copy-start.9 = (f32[512,512]{1,0:T(8,128)}, f32[512,512]{1,0:T(8,128)S(1)}, u32[]{:S(2)}) copy-start(f32[512,512]{1,0:T(8,128)S(1)} %select_select_fusion) | copy-start | bytes 3145732
  700.2 52.8 %copy-start.10 = (f32[512,512]{1,0:T(8,128)}, f32[512,512]{1,0:T(8,128)S(1)}, u32[]{:S(2)}) copy-start(f32[512,512]{1,0:T(8,128)S(1)} %get-tuple-element.251) | copy-start | bytes 3145732
  741.3 153.7 %collective-permute-start.2 = (f32[6,64,1536]{2,1,0:T(8,128)}, f32[6,64,1536]{2,1,0:T(8,128)}, u32[]{:S(2)}, u32[]{:S(2)}) collective-permute-start(f32[6,64,1536]{2,1,0:T(8,128)} %bitcast.181), channel_id=1, source_target_pairs={{0,4},{1,5},{2,6},{3,7},{4,0},{5,1},{6,2},{7,3},{8,12},{9,13},{10,... | collective-permute-start | bytes 7077896 | tf_op jit(solution)/shard_map/ppermute | solution.py:258
  741.3 286.1 %collective-permute-start.3 = (f32[6,64,1536]{2,1,0:T(8,128)}, f32[6,64,1536]{2,1,0:T(8,128)}, u32[]{:S(2)}, u32[]{:S(2)}) collective-permute-start(f32[6,64,1536]{2,1,0:T(8,128)} %bitcast.179), channel_id=1, source_target_pairs={{0,4},{1,5},{2,6},{3,7},{4,0},{5,1},{6,2},{7,3},{8,12},{9,13},{10,... | collective-permute-start | bytes 7077896 | tf_op jit(solution)/shard_map/ppermute | solution.py:258
  794.2 14.5 %copy-start.4 = (f32[128,6144]{0,1:T(8,128)S(1)}, f32[128,6144]{0,1:T(8,128)}, u32[]{:S(2)}) copy-start(f32[128,6144]{0,1:T(8,128)} %copy.109) | copy-start | bytes 9437188
  802.6 6.1 copy-start.2
  809.6 89.6 %copy-start.1 = (f32[512,6144]{0,1:T(8,128)}, f32[512,6144]{0,1:T(8,128)S(1)}, u32[]{:S(2)}) copy-start(f32[512,6144]{0,1:T(8,128)S(1)} %pad_maximum_fusion) | copy-start | bytes 37748740
  809.6 90.9 %copy-start.16 = (f32[4096]{0:T(1024)S(1)}, f32[4096]{0:T(1024)}, u32[]{:S(2)}) copy-start(f32[4096]{0:T(1024)} %param.14) | copy-start | bytes 49156
  809.6 90.9 %copy-start.17 = (s32[2048]{0:T(1024)S(1)}, s32[2048]{0:T(1024)}, u32[]{:S(2)}) copy-start(s32[2048]{0:T(1024)} %add.279) | copy-start | bytes 24580
  809.6 90.9 %copy-start.18 = (pred[4096]{0:T(1024)(128)(4,1)S(1)}, pred[4096]{0:T(1024)(128)(4,1)}, u32[]{:S(2)}) copy-start(pred[4096]{0:T(1024)(128)(4,1)} %iota_compare_fusion.3) | copy-start | bytes 12292
  (8 other events, 23.8 us)
Sparse Core Ops, SparseCore 0:
  283.7 53.2 all-gather.5
  338.6 110.8 all-gather.3
  565.0 104.8 all-reduce.2
